TPU v7x, 256 devices: a whole 4x4x8 slice. The times are simulated.
256 devices in a mesh: pix: 32 (over z_hi, y, x), tm: 8 (over z_lo, core).
Axes of the slice: x: 4, y: 4, z: 8 (z_hi: 2, z_lo: 4; z = z_hi * 4 + z_lo), core: 2. Of those that a mesh axis runs over, the one named last changes fastest.
Arguments:
- fields: float32 [256, 8, 2, 1024], P('pix', None, None, 'tm'), may hold values from -6 to 6
- profiles: bfloat16 [65536, 256], P('pix'), may hold values from -0.75 to 0.75
- phase: float32 [256, 1024], P(('pix', 'tm')), may hold values from -3.140625 to 3.140625
Outputs:
- advanced: float32 [256, 8, 2, 1024], P('pix', None, None, 'tm')
All inputs are finite; a program needn't handle non-finite values.
Results may differ from a plain program's by a relative error of at most 0.003.
Values may be sent and summed in bfloat16 or wider, within the bound.
A program may use at most 64 MiB of HBM per device.

v0:
```python
import math

import jax
import jax.numpy as jnp
from jax import lax
from jax.sharding import PartitionSpec as P


def joined_along(blocks, dim):
    blocks = jnp.moveaxis(blocks, 0, dim)
    dims = blocks.shape
    return blocks.reshape(*dims[:dim], dims[dim] * dims[dim + 1], *dims[dim + 2 :])


def copy_for_each(value, axis):
    devices = lax.axis_size(axis)
    return lax.all_to_all(
        jnp.broadcast_to(value[None], (devices, *value.shape)), axis, 0, 0, tiled=True
    )


def gathered_copies(value, axis, dim):
    return joined_along(copy_for_each(value, axis), dim)


def in_blocks(value, dim, devices):
    dims = value.shape
    blocks = value.reshape(*dims[:dim], devices, dims[dim] // devices, *dims[dim + 1 :])
    return jnp.moveaxis(blocks, dim, 0)


def summed_on_arrival(value, axis, dim):
    blocks = in_blocks(value, dim, lax.axis_size(axis))
    arrived = lax.all_to_all(blocks, axis, split_axis=0, concat_axis=0, tiled=True)
    return arrived.astype(jnp.float32).sum(axis=0)


def split_length(length):
    first = 2 ** ((length.bit_length() - 1) // 2)
    return (first, length // first)


def small_table(size):
    index = jnp.arange(size, dtype=jnp.int32)
    product = index[:, None] * index[None, :] % size
    angles = product.astype(jnp.float32) * (2.0 * math.pi / size)
    return (jnp.cos(angles), jnp.sin(angles))


def twiddles(first, second, length):
    rows = jnp.arange(first, dtype=jnp.int32)
    cols = jnp.arange(second, dtype=jnp.int32)
    product = rows[:, None] * cols[None, :] % length
    angles = product.astype(jnp.float32) * (2.0 * math.pi / length)
    return (jnp.cos(angles), jnp.sin(angles))


def contract_last(values, table):
    return jnp.einsum(
        "mbkv,vq->mbkq",
        values,
        table,
        precision=lax.Precision.HIGHEST,
        preferred_element_type=jnp.float32,
    )


def contract_third(values, table):
    return jnp.einsum(
        "mbuv,uk->mbkv",
        values,
        table,
        precision=lax.Precision.HIGHEST,
        preferred_element_type=jnp.float32,
    )


def dispersed(values, phase_rows, length):
    first, second = split_length(length)
    cos_first, sin_first = small_table(first)
    cos_second, sin_second = small_table(second)
    twist_cos, twist_sin = twiddles(first, second, length)
    modes_here = values.shape[0]
    batch = values.shape[1]
    real_part = values[:, :, 0].reshape(modes_here, batch, first, second)
    imag_part = values[:, :, 1].reshape(modes_here, batch, first, second)
    section_re = contract_third(real_part, cos_first) + contract_third(imag_part, sin_first)
    section_im = contract_third(imag_part, cos_first) - contract_third(real_part, sin_first)
    turned_re = section_re * twist_cos + section_im * twist_sin
    turned_im = section_im * twist_cos - section_re * twist_sin
    freq_re = contract_last(turned_re, cos_second) + contract_last(turned_im, sin_second)
    freq_im = contract_last(turned_im, cos_second) - contract_last(turned_re, sin_second)
    ordered = jnp.transpose(phase_rows.reshape(modes_here, second, first), (0, 2, 1))[:, None]
    phase_cos = jnp.cos(ordered)
    phase_sin = jnp.sin(ordered)
    spun_re = freq_re * phase_cos - freq_im * phase_sin
    spun_im = freq_re * phase_sin + freq_im * phase_cos
    back_re = contract_last(spun_re, cos_second) - contract_last(spun_im, sin_second)
    back_im = contract_last(spun_im, cos_second) + contract_last(spun_re, sin_second)
    again_re = back_re * twist_cos - back_im * twist_sin
    again_im = back_im * twist_cos + back_re * twist_sin
    out_re = contract_third(again_re, cos_first) - contract_third(again_im, sin_first)
    out_im = contract_third(again_im, cos_first) + contract_third(again_re, sin_first)
    out_re = out_re.reshape(modes_here, batch, length) / length
    out_im = out_im.reshape(modes_here, batch, length) / length
    return jnp.stack([out_re, out_im], axis=2)


def body(fields, profiles, phase):
    mode_local = fields.shape[0]
    batch = fields.shape[1]
    time_local = fields.shape[3]
    pixel_local = profiles.shape[0]
    length = time_local * lax.axis_size("tm")
    scale = 1.0 / math.sqrt(pixel_local * lax.axis_size("pix"))
    modal = fields.astype(jnp.bfloat16)
    piece = gathered_copies(modal, "pix", 0)
    columns = profiles
    spatial = jnp.dot(
        columns, piece.reshape(piece.shape[0], -1), preferred_element_type=jnp.float32
    )
    spatial = spatial.reshape(pixel_local, batch, 2, time_local)
    real_part = spatial[:, :, 0]
    imag_part = spatial[:, :, 1]
    power = real_part * real_part + imag_part * imag_part
    nonlin = (
        jnp.stack([power * real_part, power * imag_part], axis=2)
        .astype(jnp.bfloat16)
        .reshape(pixel_local, -1)
    )
    columns = profiles
    kerr = summed_on_arrival(
        lax.dot_general(
            columns, nonlin, (((0,), (0,)), ((), ())), preferred_element_type=jnp.float32
        ).astype(jnp.bfloat16),
        "pix",
        0,
    )
    kerr = kerr.reshape(mode_local, batch, 2, time_local) * scale
    stepped = jnp.stack([fields[:, :, 0] - kerr[:, :, 1], fields[:, :, 1] + kerr[:, :, 0]], axis=2)
    result = dispersed(
        lax.all_to_all(stepped, "tm", split_axis=0, concat_axis=3, tiled=True), phase, length
    )
    return lax.all_to_all(result, "tm", split_axis=3, concat_axis=0, tiled=True)


def solution(mesh):
    return jax.shard_map(
        body,
        mesh=mesh,
        in_specs=(P("pix", None, None, "tm"), P("pix", None), P(("pix", "tm"), None)),
        out_specs=P("pix", None, None, "tm"),
        check_vma=False,
    )
```

profile of v0, /device:TPU:1, one launch (start us, length us, event | category | flops | bytes accessed | tf_op | source)
XLA Modules:
  0.0 126.4 jit_solution(6760236970866442374)
XLA Ops:
  0.0 1.0 convert_element_type.76
  1.0 0.9 broadcast_in_dim.2
  1.9 35.3 %all_to_all.46 = bf16[32,8,8,2,128]{4,3,2,1,0:T(2,128)(2,1)S(1)} all-to-all(bf16[32,8,8,2,128]{4,3,2,1,0:T(2,128)(2,1)S(1)} %broadcast_in_dim.2), channel_id=1, replica_groups=mesh['pix'=32,'tm'=8] {'pix'}, dimensions={0} | all-to-all | bytes 2097152 | tf_op jit(solution)/shard_map/all_to_all | solution.py:17
  37.2 0.8 reshape_reshape.3
  38.0 0.5 copy.59
  38.6 2.4 %fusion.7 = f32[2048,8,2,128]{0,3,2,1:T(8,128)S(1)} fusion(bf16[8,2,128,256]{3,2,1,0:T(8,128)(2,1)S(1)} %bitcast.110, bf16[2048,256]{1,0:T(8,128)(2,1)S(1)} %copy-done), kind=kOutput, calls=%fused_computation.21 | convolution fusion | flops 2147483648 | bytes 18874368 | tf_op jit(solution)/shard_map/dot_general | solution.py:119
  40.9 3.7 %multiply_convert_fusion.1 = (bf16[2048,8,1,128]{0,3,2,1:T(8,128)(2,1)S(1)}, bf16[2048,8,1,128]{0,3,2,1:T(8,128)(2,1)}) fusion(f32[2048,8,2,128]{0,3,2,1:T(8,128)S(1)} %fusion.7), kind=kLoop, calls=%fused_computation.2 | loop fusion | flops 14680064 | bytes 25165824 | tf_op jit(solution)/shard_map/convert
  44.7 6.2 %pad_maximum_fusion = bf16[2048,8,2,128]{0,3,2,1:T(8,128)(2,1)} fusion(bf16[2048,8,1,128]{0,3,2,1:T(8,128)(2,1)} %get-tuple-element.10, bf16[2048,8,1,128]{0,3,2,1:T(8,128)(2,1)S(1)} %get-tuple-element.9), kind=kLoop, calls=%fused_computation | loop fusion | flops 4194304 | bytes 16777216 | tf_op jit(solution)/shard_map/stack | solution.py:127
  50.8 6.9 %fusion = bf16[32,8,2048]{2,1,0:T(8,128)(2,1)} fusion(bf16[2048,2048]{0,1:T(8,128)(2,1)} %bitcast.109, bf16[2048,256]{1,0:T(8,128)(2,1)S(1)} %copy-done), kind=kOutput, calls=%fused_computation.5 | convolution fusion | flops 2148007936 | bytes 10485760 | tf_op jit(solution)/shard_map/dot_general | solution.py:133
  57.7 4.5 %all-to-all-start.1 = ((bf16[32,8,2048]{2,1,0:T(8,128)(2,1)}), bf16[32,8,2048]{2,1,0:T(8,128)(2,1)S(1)}, u32[]{:S(2)}, u32[]{:S(2)}) async-start(bf16[32,8,2048]{2,1,0:T(8,128)(2,1)} %fusion), calls=%async_computation.1 | async-start | bytes 2097152 | tf_op jit(solution)/shard_map/all_to_all | solution.py:34
  62.3 15.6 %all-to-all-done.1 = bf16[32,8,2048]{2,1,0:T(8,128)(2,1)S(1)} async-done(((bf16[32,8,2048]{2,1,0:T(8,128)(2,1)}), bf16[32,8,2048]{2,1,0:T(8,128)(2,1)S(1)}, u32[]{:S(2)}, u32[]{:S(2)}) %all-to-all-start.1) | async-done | bytes 1048608 | tf_op jit(solution)/shard_map/all_to_all | solution.py:34
  78.2 0.7 pad_maximum_fusion.1
  78.9 21.8 %all-to-all-start.2 = ((f32[8,8,2,128]{3,2,1,0:T(2,128)}), f32[8,8,2,128]{3,2,1,0:T(2,128)S(1)}, u32[]{:S(2)}, u32[]{:S(2)}) async-start(f32[8,8,2,128]{3,2,1,0:T(2,128)} %pad_maximum_fusion.1), calls=%async_computation.2 | async-start | bytes 131072 | tf_op jit(solution)/shard_map/all_to_all | solution.py:142
  101.4 4.4 %all-to-all-done.2 = f32[8,8,2,128]{3,2,1,0:T(2,128)S(1)} async-done(((f32[8,8,2,128]{3,2,1,0:T(2,128)}), f32[8,8,2,128]{3,2,1,0:T(2,128)S(1)}, u32[]{:S(2)}, u32[]{:S(2)}) %all-to-all-start.2) | async-done | bytes 65568 | tf_op jit(solution)/shard_map/all_to_all | solution.py:142
  110.3 0.4 fusion.17
  111.5 0.4 fusion.6
  112.0 0.5 copy.75
  112.5 1.6 %reshape.213 = f32[8,1,2048]{2,1,0:T(1,128)S(1)} reshape(f32[1024,1,2,8]{3,2,1,0:T(2,128)S(1)} %bitcast.112) | data formatting | bytes 131072
  114.1 8.3 %all_to_all.47 = f32[8,1,2048]{2,1,0:T(1,128)S(1)} all-to-all(f32[8,1,2048]{2,1,0:T(1,128)S(1)} %reshape.213), channel_id=1, replica_groups=mesh['pix'=32,'tm'=8] {'tm'}, dimensions={0} | all-to-all | bytes 131072 | tf_op jit(solution)/shard_map/all_to_all | solution.py:144
  122.4 0.5 broadcast.240
  122.9 0.8 reduce.12
  123.7 1.6 %reshape.214 = f32[1024,1,2,8]{3,2,1,0:T(2,128)S(1)} reshape(f32[8,2048]{1,0:T(8,128)S(1)} %reduce.12) | data formatting | bytes 131072
  125.3 0.4 copy.76
  125.8 0.7 copy.77
  (40 shorter events, 6.4 us)
Async XLA Ops:
  0.0 38.5 %copy-start = (bf16[2048,256]{1,0:T(8,128)(2,1)S(1)}, bf16[2048,256]{1,0:T(8,128)(2,1)}, u32[]{:S(2)}) copy-start(bf16[2048,256]{1,0:T(8,128)(2,1)} %param.4) | copy-start | bytes 3145732
  50.8 27.3 %copy-start.1 = (f32[8,8,2,128]{3,2,1,0:T(2,128)S(1)}, f32[8,8,2,128]{3,2,1,0:T(2,128)}, u32[]{:S(2)}) copy-start(f32[8,8,2,128]{3,2,1,0:T(2,128)} %param.3) | copy-start | bytes 196612
  50.8 50.1 %copy-start.2 = (f32[1,1024]{1,0:T(1,128)S(1)}, f32[1,1024]{1,0:T(1,128)}, u32[]{:S(2)}) copy-start(f32[1,1024]{1,0:T(1,128)} %param.5) | copy-start | bytes 12292
  57.7 20.2 %all-to-all-start.1 = ((bf16[32,8,2048]{2,1,0:T(8,128)(2,1)}), bf16[32,8,2048]{2,1,0:T(8,128)(2,1)S(1)}, u32[]{:S(2)}, u32[]{:S(2)}) async-start(bf16[32,8,2048]{2,1,0:T(8,128)(2,1)} %fusion), calls=%async_computation.1 | async-start | bytes 2097152 | tf_op jit(solution)/shard_map/all_to_all | solution.py:34
  78.9 26.9 %all-to-all-start.2 = ((f32[8,8,2,128]{3,2,1,0:T(2,128)}), f32[8,8,2,128]{3,2,1,0:T(2,128)S(1)}, u32[]{:S(2)}, u32[]{:S(2)}) async-start(f32[8,8,2,128]{3,2,1,0:T(2,128)} %pad_maximum_fusion.1), calls=%async_computation.2 | async-start | bytes 131072 | tf_op jit(solution)/shard_map/all_to_all | solution.py:142
where the time goes:
time: 127 us; the launch traced here: 126 us
  blocking collectives  43.6 us (34%)
  starting transfers between devices  26.3 us (21%)
  waiting for transfers between devices  20 us (16%)
  matrix products  14.7 us (12%)
  other arithmetic  12.7 us (10%)
  local copies, waits for them, and re-layouts  8.85 us (7%)
    all_to_all x1, blocking collectives, copy_for_each(): lax.all_to_all(jnp.broadcast_to(value[None], (devices, *value.shape)), ax...  35.3 us
    all_to_all x1, starting transfers between devices, body(): lax.all_to_all(stepped, 'tm', split_axis=0, concat_axis=3, tiled=True)  21.8 us
    all_to_all x1, waiting for transfers between devices, summed_on_arrival(): lax.all_to_all(blocks, axis, split_axis=0, concat_axis=0, tiled=True)  15.6 us
    all_to_all x1, blocking collectives, body(): return lax.all_to_all(result, 'tm', split_axis=3, concat_axis=0, tiled=True)  8.29 us
    dot_general x1, matrix products, body(): lax.dot_general(columns, nonlin, (((0,), (0,)), ((), ())), preferred_elem...  6.85 us
    another operation x1, other arithmetic, body(): jnp.stack([power * real_part, power * imag_part], axis=2)  6.18 us
    all_to_all x1, starting transfers between devices, summed_on_arrival(): lax.all_to_all(blocks, axis, split_axis=0, concat_axis=0, tiled=True)  4.52 us
    all_to_all x1, waiting for transfers between devices, body(): lax.all_to_all(stepped, 'tm', split_axis=0, concat_axis=3, tiled=True)  4.38 us
  transfers between devices with their start and end apart: 2, of which 2 were waited for; matrix products, arithmetic and copies ran while one was open for 1% of the time, Pallas kernels for 0%

commit v1 on v0

v1 whole, which is shorter than its diff:
```python
import functools
import math

import jax
import jax.numpy as jnp
import numpy as np
from jax import lax
from jax.experimental import pallas as pl
from jax.experimental.pallas import tpu as pltpu
from jax.sharding import PartitionSpec as P

MESH = pl.DeviceIdType.MESH
F32 = jnp.float32
BF16 = jnp.bfloat16

SLOTS = ((2, 0), (2, 1), (1, 0), (1, 1), (3, 0), (3, 1), (0, 1), (0, 0))
TILE = 512


def tables():
    row = np.arange(256)
    order = (row // 8 % 2) * 128 + (row // 16) * 8 + row % 8
    perm = np.zeros((256, 256), np.float32)
    perm[order, row] = 1.0
    angle = 2.0 * np.pi * (np.outer(np.arange(128), np.arange(128)) % 128) / 128.0
    cos, sin = np.cos(angle), np.sin(angle)
    dft = np.block([[cos, -sin], [sin, cos]]).astype(np.float32)
    high = dft.astype(jnp.bfloat16)
    low = (dft - high.astype(np.float32)).astype(jnp.bfloat16)
    turn = 2.0 * np.pi * np.outer(np.arange(8), np.arange(128)) / 1024.0
    twist = np.concatenate([np.cos(turn), np.sin(turn)]).astype(np.float32)
    square = np.stack([perm.astype(jnp.bfloat16), high, low])
    return square, twist


def fft8(re, im, sign):
    half = math.sqrt(0.5)

    def turned(x, y, k):
        if k == 0:
            return x, y
        if k == 1:
            return (x - sign * y) * half, (y + sign * x) * half
        if k == 2:
            return (-y, x) if sign > 0 else (y, -x)
        return (-x - sign * y) * half, (-y + sign * x) * half

    def four(r, i):
        ar, ai, br, bi = r[0] + r[2], i[0] + i[2], r[0] - r[2], i[0] - i[2]
        cr, ci, dr, di = r[1] + r[3], i[1] + i[3], r[1] - r[3], i[1] - i[3]
        dr, di = turned(dr, di, 2)
        return [ar + cr, br + dr, ar - cr, br - dr], [ai + ci, bi + di, ai - ci, bi - di]

    er, ei = four(re[0::2], im[0::2])
    od, oi = four(re[1::2], im[1::2])
    out_re, out_im = [None] * 8, [None] * 8
    for k in range(4):
        tr, ti = turned(od[k], oi[k], k)
        out_re[k], out_im[k] = er[k] + tr, ei[k] + ti
        out_re[k + 4], out_im[k + 4] = er[k] - tr, ei[k] - ti
    return out_re, out_im


def split(value):
    high = value.astype(BF16)
    return high, (value - high.astype(F32)).astype(BF16)


def dot(a, b, dims=((1,), (0,))):
    return lax.dot_general(a, b, (dims, ((), ())), preferred_element_type=F32)


def kernel(
    f_hbm, p_hbm, ph_hbm, sq_hbm, tw_hbm, o_ref,
    f_v, p_v, ph_v, sq_v, tw_v, pm_v, pt_v, mbuf, s_hi, s_lo, a1, lo, cs_s, cs_r,
    kf, ks, kr1, kown, k1s, kr2, kmid, kx, esf, esb, erf, erb,
    in_sem, a1s, a1r, los, lor, css, csr, a2s, a2r, c1s, c1r, efs, efr, ebs, ebr,
):
    pix, tm = lax.axis_index("pix"), lax.axis_index("tm")
    zh, y, x = pix // 16, (pix // 4) % 4, pix % 4
    yx = pix % 16
    zl, core = tm // 2, tm % 2
    other = 1 - zh
    here = zh * 8 + tm

    def at_z(h, t):
        return (h * 16 + yx, t)

    def at_x(k):
        return (zh * 16 + y * 4 + lax.rem(x + k, 4), tm)

    def at_y(k):
        return (zh * 16 + lax.rem(y + k, 4) * 4 + x, tm)

    def remote(src, dst, ss, rs, device):
        return pltpu.make_async_remote_copy(
            src_ref=src, dst_ref=dst, send_sem=ss, recv_sem=rs, device_id=device, device_id_type=MESH
        )

    def column(o):
        peer = lax.rem(here + o, 16)
        return peer // 8, lax.rem(peer, 8)

    sends = []

    def send(*a):
        copy = remote(*a)
        copy.start()
        sends.append(copy)

    def arrive(ref, rs):
        remote(ref, ref, rs, rs, at_x(1)).wait_recv()

    barrier = pltpu.get_barrier_semaphore()
    for o in range(1, 16):
        h, t = column(o)
        pl.semaphore_signal(barrier, inc=1, device_id=at_z(h, t), device_id_type=MESH)
    for k in range(1, 4):
        pl.semaphore_signal(barrier, inc=1, device_id=at_x(k), device_id_type=MESH)
        pl.semaphore_signal(barrier, inc=1, device_id=at_y(k), device_id_type=MESH)

    loads = [
        pltpu.make_async_copy(src, dst, in_sem.at[n])
        for n, (src, dst) in enumerate(
            ((f_hbm, f_v), (ph_hbm, ph_v), (sq_hbm, sq_v), (p_hbm, p_v), (tw_hbm, tw_v))
        )
    ]
    for load in loads:
        load.start()

    loads[0].wait()
    for b in range(8):
        value = jnp.concatenate([f_v[pl.ds(2 * b + c, 8, stride=16), :] for c in range(2)], axis=0)
        high, low = split(value)
        s_hi[b] = high
        s_lo[b] = low
    a1[here] = s_hi[tm]
    lo[tm] = s_lo[tm]

    pl.semaphore_wait(barrier, 21)
    for o in (8, 7, 9, 6, 10, 5, 11, 4, 12, 3, 13, 2, 14, 1, 15):
        h, t = column(o)
        send(s_hi.at[t], a1.at[here], a1s.at[o], a1r.at[here], at_z(h, t))

    loads[1].wait()
    lane = lax.broadcasted_iota(jnp.int32, (8, 128), 1)
    sub = lax.broadcasted_iota(jnp.int32, (8, 128), 0)
    chosen = lax.rem(lane, 8) == sub
    rows = []
    for k in range(8):
        spread = jnp.where(chosen, jnp.broadcast_to(ph_v[k : k + 1, :], (8, 128)), 0.0)
        first, rest = split(spread)
        second = rest.astype(F32)
        third = spread - first.astype(F32) - second
        rows += [first.astype(F32), second, third]
    gather_lane = lax.broadcasted_iota(jnp.int32, (128, 128), 0) // 8
    gather = (gather_lane == lax.broadcasted_iota(jnp.int32, (128, 128), 1)).astype(F32).astype(BF16)
    packed = dot(jnp.concatenate(rows, axis=0).astype(BF16), gather)
    angle = jnp.zeros((8, 128), F32)
    for k in range(8):
        part = packed[24 * k : 24 * k + 8] + packed[24 * k + 8 : 24 * k + 16] + packed[24 * k + 16 : 24 * k + 24]
        angle = angle + (part if k == 0 else pltpu.roll(part, 16 * k, 1))
    cs_s[0:8, :] = jnp.cos(angle)
    cs_s[8:16, :] = jnp.sin(angle)
    mine = pl.ds(pl.multiple_of(here * 16, 16), 16)
    cs_r[mine, :] = cs_s[...]
    for o in range(1, 8):
        t = lax.rem(tm + o, 8)
        send(s_lo.at[t], lo.at[tm], los.at[o], lor.at[tm], at_z(zh, t))
    for o in range(1, 16):
        h, t = column(o)
        send(cs_s, cs_r.at[mine], css.at[o], csr.at[here], at_z(h, t))

    loads[2].wait()
    loads[3].wait()
    for n in range(2048 // TILE):
        block = p_v[n * TILE : (n + 1) * TILE, :]
        pm_v[n] = dot(block, sq_v[0]).astype(BF16)
        pt_v[n] = dot(sq_v[0], block, ((0,), (1,))).astype(BF16)

    blocks = [lax.rem(zl + step, 4) * 2 + lax.rem(core + c, 2) for step, c in SLOTS]

    for n, a in enumerate(blocks):
        if SLOTS[n] != (0, 0):
            arrive(a1.at[zh * 8 + a], a1r.at[zh * 8 + a])
        arrive(a1.at[other * 8 + a], a1r.at[other * 8 + a])
        first, second = a1[a].astype(F32), a1[8 + a].astype(F32)
        for c in range(2):
            both = jnp.concatenate([first[8 * c : 8 * c + 8], second[8 * c : 8 * c + 8]], axis=0)
            mbuf[a, c, y, x] = both.astype(BF16)
        piece = mbuf.at[a, :, y, x]
        for k in range(1, 4):
            send(piece, piece, a2s.at[n, k - 1], a2r.at[n, k - 1], at_x(k) if n % 2 == 0 else at_y(k))

    def second_leg(n):
        a = blocks[n]
        for k in range(1, 4):
            at = (y, lax.rem(x + 4 - k, 4)) if n % 2 == 0 else (lax.rem(y + 4 - k, 4), x)
            arrive(mbuf.at[a, :, at[0], at[1]], a2r.at[n, k - 1])
        piece = mbuf.at[a, :, y] if n % 2 == 0 else mbuf.at[a, :, :, x]
        for k in range(1, 4):
            send(piece, piece, a2s.at[n, k + 2], a2r.at[n, k + 2], at_y(k) if n % 2 == 0 else at_x(k))

    def compute(n):
        a = blocks[n]
        for k in range(1, 4):
            if n % 2 == 0:
                piece = mbuf.at[a, :, lax.rem(y + 4 - k, 4)]
            else:
                piece = mbuf.at[a, :, :, lax.rem(x + 4 - k, 4)]
            arrive(piece, a2r.at[n, k + 2])
        fields = jnp.concatenate([mbuf[a, c].reshape(256, 128) for c in range(2)], axis=1)
        total = None
        for t in range(2048 // TILE):
            spatial = dot(pm_v[t], fields)
            re, im = spatial[:, :128], spatial[:, 128:]
            power = re * re + im * im
            nonlin = jnp.concatenate([power * re, power * im], axis=1).astype(BF16)
            part = dot(pt_v[t], nonlin)
            total = part if total is None else total + part
        for c in range(2):
            half = total[:, 128 * c : 128 * c + 128].reshape(4, 4, 16, 128)
            kf[n, c] = half
            ks[n, c] = half.astype(BF16)
        for k in range(1, 4):
            if n % 2 == 0:
                piece, to = ks.at[n, :, :, lax.rem(x + k, 4)], at_x(k)
            else:
                piece, to = ks.at[n, :, lax.rem(y + k, 4)], at_y(k)
            send(piece, kr1.at[n, k - 1], c1s.at[n, k - 1], c1r.at[n, k - 1], to)

    def reduce_first(n):
        for k in range(3):
            arrive(kr1.at[n, k], c1r.at[n, k])
        total = kf[n, :, :, x] if n % 2 == 0 else kf[n, :, y]
        for k in range(3):
            total = total + kr1[n, k].astype(F32)
        kmid[n] = total
        k1s[n] = total.astype(BF16)
        for k in range(1, 4):
            if n % 2 == 0:
                piece, to = k1s.at[n, :, lax.rem(y + k, 4)], at_y(k)
            else:
                piece, to = k1s.at[n, :, lax.rem(x + k, 4)], at_x(k)
            send(piece, kr2.at[n, k - 1], c1s.at[n, k + 2], c1r.at[n, k + 2], to)

    def reduce_second(n):
        for k in range(3):
            arrive(kr2.at[n, k], c1r.at[n, k + 3])
        total = kmid[n, :, y] if n % 2 == 0 else kmid[n, :, x]
        for k in range(3):
            total = total + kr2[n, k].astype(F32)
        kx[blocks[n]] = total

    second_leg(0)
    second_leg(1)
    for n in range(8):
        if n + 2 < 8:
            second_leg(n + 2)
        compute(n)
        if n >= 3:
            reduce_first(n - 3)
        if n >= 6:
            reduce_second(n - 6)
    for n in range(5, 8):
        reduce_first(n)
        reduce_second(n - 3)
    for n in range(5, 8):
        reduce_second(n)

    loads[4].wait()
    for o in range(1, 8):
        t = lax.rem(tm + o, 8)
        arrive(lo.at[t], lor.at[t])
    for o in range(1, 16):
        h, t = column(o)
        peer = h * 8 + t
        arrive(cs_r.at[pl.ds(pl.multiple_of(peer * 16, 16), 16)], csr.at[peer])
    scale = 1.0 / math.sqrt(65536.0)
    at_low = jnp.where(zh == 0, 1.0, 0.0).astype(F32)
    at_high = 1.0 - at_low
    step_re, step_im = [], []
    for a in range(8):
        own = a1[zh * 8 + a].astype(F32) + lo[a].astype(F32)
        own_re = jnp.concatenate([own[:8] * at_low, own[:8] * at_high], axis=0)
        own_im = jnp.concatenate([own[8:] * at_low, own[8:] * at_high], axis=0)
        step_re.append(own_re - kx[a, 1] * scale)
        step_im.append(own_im + kx[a, 0] * scale)
    fre, fim = fft8(step_re, step_im, -1)
    turned = []
    for r in range(8):
        cos, sin = tw_v[r : r + 1, :], tw_v[8 + r : 9 + r, :]
        turned.append(jnp.concatenate([fre[r] * cos + fim[r] * sin, fim[r] * cos - fre[r] * sin], axis=1))
    high, low = split(jnp.concatenate(turned, axis=0))
    freq = dot(high, sq_v[1]) + dot(low, sq_v[1]) + dot(high, sq_v[2])
    spun = []
    for r in range(8):
        cos, sin = cs_r[pl.ds(r, 16, stride=16), :], cs_r[pl.ds(8 + r, 16, stride=16), :]
        re, im = freq[16 * r : 16 * r + 16, :128], freq[16 * r : 16 * r + 16, 128:]
        spun.append(jnp.concatenate([re * cos - im * sin, re * sin + im * cos], axis=1))
    high, low = split(jnp.concatenate(spun, axis=0))
    back_dims = ((1,), (1,))
    back = dot(high, sq_v[1], back_dims) + dot(low, sq_v[1], back_dims) + dot(high, sq_v[2], back_dims)
    again_re, again_im = [], []
    for r in range(8):
        cos, sin = tw_v[r : r + 1, :] * (1.0 / 1024.0), tw_v[8 + r : 9 + r, :] * (1.0 / 1024.0)
        re, im = back[16 * r : 16 * r + 16, :128], back[16 * r : 16 * r + 16, 128:]
        again_re.append(re * cos - im * sin)
        again_im.append(im * cos + re * sin)
    out_re, out_im = fft8(again_re, again_im, 1)

    for a in range(8):
        low_half = jnp.concatenate([out_re[a][:8], out_im[a][:8]], axis=0)
        high_half = jnp.concatenate([out_re[a][8:], out_im[a][8:]], axis=0)
        esf[a] = low_half * at_low + high_half * at_high
        esb[a] = (low_half * at_high + high_half * at_low).astype(BF16)
    for o in range(8):
        t = lax.rem(tm + o, 8)
        send(esb.at[t], erb.at[tm], ebs.at[o], ebr.at[tm], at_z(other, t))
    for o in range(1, 8):
        t = lax.rem(tm + o, 8)
        send(esf.at[t], erf.at[tm], efs.at[o], efr.at[tm], at_z(zh, t))
    erf[tm] = esf[tm]
    for o in range(8):
        t = lax.rem(tm + o, 8)
        if o:
            arrive(erf.at[t], efr.at[t])
        arrive(erb.at[t], ebr.at[t])
    for b in range(8):
        value = erf[b] + erb[b].astype(F32)
        for c in range(2):
            o_ref[pl.ds(2 * b + c, 8, stride=16), :] = value[8 * c : 8 * c + 8]
    for copy in sends:
        copy.wait_send()


def body(fields, profiles, phase):
    square, twist = tables()
    dma = pltpu.SemaphoreType.DMA
    any_spec = pl.BlockSpec(memory_space=pl.ANY)
    out = pl.pallas_call(
        kernel,
        out_shape=jax.ShapeDtypeStruct((128, 128), F32),
        in_specs=[any_spec] * 5,
        out_specs=pl.BlockSpec(memory_space=pltpu.VMEM),
        scratch_shapes=[
            pltpu.VMEM((128, 128), F32),
            pltpu.VMEM((2048, 256), BF16),
            pltpu.VMEM((8, 128), F32),
            pltpu.VMEM((3, 256, 256), BF16),
            pltpu.VMEM((16, 128), F32),
            pltpu.VMEM((2048 // TILE, TILE, 256), BF16),
            pltpu.VMEM((2048 // TILE, 256, TILE), BF16),
            pltpu.VMEM((8, 2, 4, 4, 16, 128), BF16),
            pltpu.VMEM((8, 16, 128), BF16),
            pltpu.VMEM((8, 16, 128), BF16),
            pltpu.VMEM((16, 16, 128), BF16),
            pltpu.VMEM((8, 16, 128), BF16),
            pltpu.VMEM((16, 128), F32),
            pltpu.VMEM((256, 128), F32),
            pltpu.VMEM((8, 2, 4, 4, 16, 128), F32),
            pltpu.VMEM((8, 2, 4, 4, 16, 128), BF16),
            pltpu.VMEM((8, 3, 2, 4, 16, 128), BF16),
            pltpu.VMEM((8, 128), F32),
            pltpu.VMEM((8, 2, 4, 16, 128), BF16),
            pltpu.VMEM((8, 3, 2, 16, 128), BF16),
            pltpu.VMEM((8, 2, 4, 16, 128), F32),
            pltpu.VMEM((8, 2, 16, 128), F32),
            pltpu.VMEM((8, 16, 128), F32),
            pltpu.VMEM((8, 16, 128), BF16),
            pltpu.VMEM((8, 16, 128), F32),
            pltpu.VMEM((8, 16, 128), BF16),
            dma((5,)),
            dma((16,)), dma((16,)),
            dma((8,)), dma((8,)),
            dma((16,)), dma((16,)),
            dma((8, 6)), dma((8, 6)),
            dma((8, 6)), dma((8, 6)),
            dma((8,)), dma((8,)),
            dma((8,)), dma((8,)),
        ],
        compiler_params=pltpu.CompilerParams(
            collective_id=0, has_side_effects=True, vmem_limit_bytes=40 * 1024 * 1024
        ),
    )(fields.reshape(128, 128), profiles, phase.reshape(8, 128), jnp.asarray(square), jnp.asarray(twist))
    return out.reshape(8, 8, 2, 128)


def solution(mesh):
    return jax.shard_map(
        body,
        mesh=mesh,
        in_specs=(P("pix", None, None, "tm"), P("pix", None), P(("pix", "tm"), None)),
        out_specs=P("pix", None, None, "tm"),
        check_vma=False,
    )
```

time: 127 us -> 59.7 us (0.47)
  Pallas kernels: 0 us -> 54.4 us
  blocking collectives: 43.6 us -> 0 us
  starting transfers between devices: 26.3 us -> 0 us
  waiting for transfers between devices: 20 us -> 0 us
  matrix products: 14.7 us -> 0 us
  other arithmetic: 12.7 us -> 0 us
  local copies, waits for them, and re-layouts: 8.85 us -> 5.07 us
    pallas_call x0 -> x1, Pallas kernels: none -> 54.4 us  [body(): pl.pallas_call(kernel, out_shape=jax.ShapeDtypeStruct((128, 128), F32), i...]
    all_to_all x2 -> x0, blocking collectives: 43.6 us -> none  [the longest x1 35.3 us: copy_for_each(): lax.all_to_all(jnp.broadcast_to(value[None], (devices, *value.shape)), ax...]
    all_to_all x2 -> x0, starting transfers between devices: 26.3 us -> none  [the longest x1 21.8 us: body(): lax.all_to_all(stepped, 'tm', split_axis=0, concat_axis=3, tiled=True)]
    all_to_all x2 -> x0, waiting for transfers between devices: 20 us -> none  [the longest x1 15.6 us: summed_on_arrival(): lax.all_to_all(blocks, axis, split_axis=0, concat_axis=0, tiled=True)]
    dot_general x18 -> x0, matrix products: 14.7 us -> none  [the longest x1 6.85 us: body(): lax.dot_general(columns, nonlin, (((0,), (0,)), ((), ())), preferred_elem...]
    another operation x4 -> x0, other arithmetic: 10.6 us -> none  [the longest x1 6.18 us: body(): jnp.stack([power * real_part, power * imag_part], axis=2)]
    unnamed x8 -> x11, local copies, waits for them, and re-layouts: 3.19 us -> 5.07 us
    all_to_all x4 -> x0, local copies, waits for them, and re-layouts: 1.65 us -> none  [the longest x3 1.62 us: body(): return lax.all_to_all(result, 'tm', split_axis=3, concat_axis=0, tiled=True)]
  transfers between devices with their start and end apart: 2 -> 0, of which waited for: 2 -> 0; matrix products, arithmetic and copies ran while one was open for 1% -> 0% of each run, Pallas kernels for 0% -> 0%
where the time goes in v1:
time: 59.7 us; the launch traced here: 59.4 us
  Pallas kernels  54.4 us (91%)
  local copies, waits for them, and re-layouts  5.07 us (8%)
    pallas_call x1, Pallas kernels, body(): pl.pallas_call(kernel, out_shape=jax.ShapeDtypeStruct((128, 128), F32), i...  54.4 us
    unnamed x11, local copies, waits for them, and re-layouts  5.07 us

profile of v1, /device:TPU:1, one launch (start us, length us, event | category | flops | bytes accessed | tf_op | source)
XLA Modules:
  0.0 59.4 jit_solution(17048766689578839011)
XLA Ops:
  0.0 0.0 copy-start
  0.0 1.2 %copy-done = bf16[2048,256]{1,0:T(8,128)(2,1)S(1)} copy-done((bf16[2048,256]{1,0:T(8,128)(2,1)S(1)}, bf16[2048,256]{1,0:T(8,128)(2,1)}, u32[]{:S(2)}) %copy-start) | copy-done | bytes 1048600
  1.2 0.0 copy-start.1
  1.2 1.0 %copy-done.1 = bf16[3,256,256]{2,1,0:T(8,128)(2,1)S(1)} copy-done((bf16[3,256,256]{2,1,0:T(8,128)(2,1)S(1)}, bf16[3,256,256]{2,1,0:T(8,128)(2,1)}, u32[]{:S(2)}) %copy-start.1) | copy-done | bytes 393240
  2.2 0.0 copy-start.2
  2.2 0.8 %copy-done.2 = f32[8,8,2,128]{3,2,1,0:T(2,128)S(1)} copy-done((f32[8,8,2,128]{3,2,1,0:T(2,128)S(1)}, f32[8,8,2,128]{3,2,1,0:T(2,128)}, u32[]{:S(2)}) %copy-start.2) | copy-done | bytes 65560
  3.1 0.0 copy-start.3
  3.1 0.7 %copy-done.3 = f32[16,128]{1,0:T(8,128)S(1)} copy-done((f32[16,128]{1,0:T(8,128)S(1)}, f32[16,128]{1,0:T(8,128)}, u32[]{:S(2)}) %copy-start.3) | copy-done | bytes 8216
  3.8 0.0 copy-start.4
  3.8 0.7 %copy-done.4 = f32[1,1024]{1,0:T(1,128)S(1)} copy-done((f32[1,1024]{1,0:T(1,128)S(1)}, f32[1,1024]{1,0:T(1,128)}, u32[]{:S(2)}) %copy-start.4) | copy-done | bytes 4120
  4.4 54.4 %shard_map.55 = f32[128,128]{1,0:T(8,128)S(1)} custom-call(f32[128,128]{1,0:T(8,128)S(1)} %bitcast.4, bf16[2048,256]{1,0:T(8,128)(2,1)S(1)} %copy-done, f32[8,128]{1,0:T(8,128)S(1)} %bitcast.5, bf16[3,256,256]{2,1,0:T(8,128)(2,1)S(1)} %copy-done.1, f32[16,128]{1,0:T(8,128)S(1)} %copy-done.3), custom_call_target="tpu_custom_call" | custom-call | tf_op jit(solution)/shard_map/pallas_call | solution.py:341
  58.8 0.6 %copy.7 = f32[8,8,2,128]{3,2,1,0:T(2,128)} copy(f32[8,8,2,128]{3,2,1,0:T(2,128)S(1)} %bitcast.3) | data formatting | bytes 131072
Async XLA Ops:
  0.0 1.2 %copy-start = (bf16[2048,256]{1,0:T(8,128)(2,1)S(1)}, bf16[2048,256]{1,0:T(8,128)(2,1)}, u32[]{:S(2)}) copy-start(bf16[2048,256]{1,0:T(8,128)(2,1)} %p_hbm.1) | copy-start | bytes 3145732
  1.2 1.0 %copy-start.1 = (bf16[3,256,256]{2,1,0:T(8,128)(2,1)S(1)}, bf16[3,256,256]{2,1,0:T(8,128)(2,1)}, u32[]{:S(2)}) copy-start(bf16[3,256,256]{2,1,0:T(8,128)(2,1)} %constant.4.clone.sq_hbm) | copy-start | bytes 1179652
  2.2 0.8 %copy-start.2 = (f32[8,8,2,128]{3,2,1,0:T(2,128)S(1)}, f32[8,8,2,128]{3,2,1,0:T(2,128)}, u32[]{:S(2)}) copy-start(f32[8,8,2,128]{3,2,1,0:T(2,128)} %param.5) | copy-start | bytes 196612
  3.1 0.7 %copy-start.3 = (f32[16,128]{1,0:T(8,128)S(1)}, f32[16,128]{1,0:T(8,128)}, u32[]{:S(2)}) copy-start(f32[16,128]{1,0:T(8,128)} %constant.5.clone.tw_hbm) | copy-start | bytes 24580
  3.8 0.7 %copy-start.4 = (f32[1,1024]{1,0:T(1,128)S(1)}, f32[1,1024]{1,0:T(1,128)}, u32[]{:S(2)}) copy-start(f32[1,1024]{1,0:T(1,128)} %param.7) | copy-start | bytes 12292

commit v2 on v1

--- a/solution.py
+++ b/solution.py
@@ -73,8 +73,8 @@
 def kernel(
     f_hbm, p_hbm, ph_hbm, sq_hbm, tw_hbm, o_ref,
     f_v, p_v, ph_v, sq_v, tw_v, pm_v, pt_v, mbuf, s_hi, s_lo, a1, lo, cs_s, cs_r,
-    kf, ks, kr1, kown, k1s, kr2, kmid, kx, esf, esb, erf, erb,
-    in_sem, a1s, a1r, los, lor, css, csr, a2s, a2r, c1s, c1r, efs, efr, ebs, ebr,
+    kf, ks, kr1, k1s, kr2, kmid, kx, esf, esb, erf, erb,
+    in_sem, out_sem, a1r, lor, csr, a2r, c1r, e_sem,
 ):
     pix, tm = lax.axis_index("pix"), lax.axis_index("tm")
     zh, y, x = pix // 16, (pix // 4) % 4, pix % 4
@@ -101,15 +101,11 @@
         peer = lax.rem(here + o, 16)
         return peer // 8, lax.rem(peer, 8)
 
-    sends = []
-
     def send(*a):
-        copy = remote(*a)
-        copy.start()
-        sends.append(copy)
-
-    def arrive(ref, rs):
-        remote(ref, ref, rs, rs, at_x(1)).wait_recv()
+        remote(*a).start()
+
+    def landed(ref, sem):
+        pltpu.make_async_copy(ref, ref, sem).wait()
 
     barrier = pltpu.get_barrier_semaphore()
     for o in range(1, 16):
@@ -140,7 +136,8 @@
     pl.semaphore_wait(barrier, 21)
     for o in (8, 7, 9, 6, 10, 5, 11, 4, 12, 3, 13, 2, 14, 1, 15):
         h, t = column(o)
-        send(s_hi.at[t], a1.at[here], a1s.at[o], a1r.at[here], at_z(h, t))
+        send(s_hi.at[t], a1.at[here], out_sem.at[0], a1r.at[tm], at_z(h, t))
+
 
     loads[1].wait()
     lane = lax.broadcasted_iota(jnp.int32, (8, 128), 1)
@@ -164,51 +161,44 @@
     cs_s[8:16, :] = jnp.sin(angle)
     mine = pl.ds(pl.multiple_of(here * 16, 16), 16)
     cs_r[mine, :] = cs_s[...]
-    for o in range(1, 8):
-        t = lax.rem(tm + o, 8)
-        send(s_lo.at[t], lo.at[tm], los.at[o], lor.at[tm], at_z(zh, t))
-    for o in range(1, 16):
-        h, t = column(o)
-        send(cs_s, cs_r.at[mine], css.at[o], csr.at[here], at_z(h, t))
-
-    loads[2].wait()
-    loads[3].wait()
+
+    for n in range(2, 5):
+        loads[n].wait()
     for n in range(2048 // TILE):
         block = p_v[n * TILE : (n + 1) * TILE, :]
         pm_v[n] = dot(block, sq_v[0]).astype(BF16)
         pt_v[n] = dot(sq_v[0], block, ((0,), (1,))).astype(BF16)
 
+    for o in range(1, 8):
+        t = lax.rem(tm + o, 8)
+        send(s_lo.at[t], lo.at[tm], out_sem.at[1], lor.at[0], at_z(zh, t))
+    for o in range(1, 16):
+        h, t = column(o)
+        send(cs_s, cs_r.at[mine], out_sem.at[2], csr.at[0], at_z(h, t))
+
     blocks = [lax.rem(zl + step, 4) * 2 + lax.rem(core + c, 2) for step, c in SLOTS]
 
-    for n, a in enumerate(blocks):
-        if SLOTS[n] != (0, 0):
-            arrive(a1.at[zh * 8 + a], a1r.at[zh * 8 + a])
-        arrive(a1.at[other * 8 + a], a1r.at[other * 8 + a])
+    def first_leg(n):
+        a = blocks[n]
+        landed(a1.at[pl.ds(0, 1 if SLOTS[n] == (0, 0) else 2)], a1r.at[a])
         first, second = a1[a].astype(F32), a1[8 + a].astype(F32)
         for c in range(2):
             both = jnp.concatenate([first[8 * c : 8 * c + 8], second[8 * c : 8 * c + 8]], axis=0)
             mbuf[a, c, y, x] = both.astype(BF16)
         piece = mbuf.at[a, :, y, x]
         for k in range(1, 4):
-            send(piece, piece, a2s.at[n, k - 1], a2r.at[n, k - 1], at_x(k) if n % 2 == 0 else at_y(k))
+            send(piece, piece, out_sem.at[3], a2r.at[n, 0], at_x(k) if n % 2 == 0 else at_y(k))
 
     def second_leg(n):
         a = blocks[n]
-        for k in range(1, 4):
-            at = (y, lax.rem(x + 4 - k, 4)) if n % 2 == 0 else (lax.rem(y + 4 - k, 4), x)
-            arrive(mbuf.at[a, :, at[0], at[1]], a2r.at[n, k - 1])
+        landed(kr2.at[n], a2r.at[n, 0])
         piece = mbuf.at[a, :, y] if n % 2 == 0 else mbuf.at[a, :, :, x]
         for k in range(1, 4):
-            send(piece, piece, a2s.at[n, k + 2], a2r.at[n, k + 2], at_y(k) if n % 2 == 0 else at_x(k))
+            send(piece, piece, out_sem.at[4], a2r.at[n, 1], at_y(k) if n % 2 == 0 else at_x(k))
 
     def compute(n):
         a = blocks[n]
-        for k in range(1, 4):
-            if n % 2 == 0:
-                piece = mbuf.at[a, :, lax.rem(y + 4 - k, 4)]
-            else:
-                piece = mbuf.at[a, :, :, lax.rem(x + 4 - k, 4)]
-            arrive(piece, a2r.at[n, k + 2])
+        landed(kr1.at[n], a2r.at[n, 1])
         fields = jnp.concatenate([mbuf[a, c].reshape(256, 128) for c in range(2)], axis=1)
         total = None
         for t in range(2048 // TILE):
@@ -227,11 +217,10 @@
                 piece, to = ks.at[n, :, :, lax.rem(x + k, 4)], at_x(k)
             else:
                 piece, to = ks.at[n, :, lax.rem(y + k, 4)], at_y(k)
-            send(piece, kr1.at[n, k - 1], c1s.at[n, k - 1], c1r.at[n, k - 1], to)
+            send(piece, kr1.at[n, k - 1], out_sem.at[5], c1r.at[n, 0], to)
 
     def reduce_first(n):
-        for k in range(3):
-            arrive(kr1.at[n, k], c1r.at[n, k])
+        landed(kr1.at[n], c1r.at[n, 0])
         total = kf[n, :, :, x] if n % 2 == 0 else kf[n, :, y]
         for k in range(3):
             total = total + kr1[n, k].astype(F32)
@@ -242,40 +231,33 @@
                 piece, to = k1s.at[n, :, lax.rem(y + k, 4)], at_y(k)
             else:
                 piece, to = k1s.at[n, :, lax.rem(x + k, 4)], at_x(k)
-            send(piece, kr2.at[n, k - 1], c1s.at[n, k + 2], c1r.at[n, k + 2], to)
+            send(piece, kr2.at[n, k - 1], out_sem.at[6], c1r.at[n, 1], to)
 
     def reduce_second(n):
-        for k in range(3):
-            arrive(kr2.at[n, k], c1r.at[n, k + 3])
+        landed(kr2.at[n], c1r.at[n, 1])
         total = kmid[n, :, y] if n % 2 == 0 else kmid[n, :, x]
         for k in range(3):
             total = total + kr2[n, k].astype(F32)
         kx[blocks[n]] = total
 
-    second_leg(0)
-    second_leg(1)
     for n in range(8):
-        if n + 2 < 8:
-            second_leg(n + 2)
+        first_leg(n)
+    for n in range(6):
+        second_leg(n)
+    for n in range(8):
         compute(n)
-        if n >= 3:
-            reduce_first(n - 3)
-        if n >= 6:
-            reduce_second(n - 6)
-    for n in range(5, 8):
-        reduce_first(n)
-        reduce_second(n - 3)
-    for n in range(5, 8):
+        if n < 2:
+            second_leg(n + 6)
+        if n >= 4:
+            reduce_first(n - 4)
+    for n in range(4):
         reduce_second(n)
-
-    loads[4].wait()
-    for o in range(1, 8):
-        t = lax.rem(tm + o, 8)
-        arrive(lo.at[t], lor.at[t])
-    for o in range(1, 16):
-        h, t = column(o)
-        peer = h * 8 + t
-        arrive(cs_r.at[pl.ds(pl.multiple_of(peer * 16, 16), 16)], csr.at[peer])
+        reduce_first(n + 4)
+    for n in range(4, 8):
+        reduce_second(n)
+
+    landed(lo.at[pl.ds(0, 7)], lor.at[0])
+    landed(cs_r.at[pl.ds(0, 240)], csr.at[0])
     scale = 1.0 / math.sqrt(65536.0)
     at_low = jnp.where(zh == 0, 1.0, 0.0).astype(F32)
     at_high = 1.0 - at_low
@@ -316,32 +298,36 @@
         esb[a] = (low_half * at_high + high_half * at_low).astype(BF16)
     for o in range(8):
         t = lax.rem(tm + o, 8)
-        send(esb.at[t], erb.at[tm], ebs.at[o], ebr.at[tm], at_z(other, t))
+        send(esb.at[t], erb.at[tm], out_sem.at[7], e_sem.at[0], at_z(other, t))
     for o in range(1, 8):
         t = lax.rem(tm + o, 8)
-        send(esf.at[t], erf.at[tm], efs.at[o], efr.at[tm], at_z(zh, t))
+        send(esf.at[t], erf.at[tm], out_sem.at[8], e_sem.at[1], at_z(zh, t))
     erf[tm] = esf[tm]
-    for o in range(8):
-        t = lax.rem(tm + o, 8)
-        if o:
-            arrive(erf.at[t], efr.at[t])
-        arrive(erb.at[t], ebr.at[t])
+    landed(erb, e_sem.at[0])
+    landed(erf.at[pl.ds(0, 7)], e_sem.at[1])
     for b in range(8):
         value = erf[b] + erb[b].astype(F32)
         for c in range(2):
             o_ref[pl.ds(2 * b + c, 8, stride=16), :] = value[8 * c : 8 * c + 8]
-    for copy in sends:
-        copy.wait_send()
+    landed(a1.at[pl.ds(0, 15)], out_sem.at[0])
+    landed(lo.at[pl.ds(0, 7)], out_sem.at[1])
+    landed(cs_r.at[pl.ds(0, 240)], out_sem.at[2])
+    landed(kr2, out_sem.at[3])
+    landed(kr1, out_sem.at[4])
+    landed(kr1, out_sem.at[5])
+    landed(kr2, out_sem.at[6])
+    landed(erb, out_sem.at[7])
+    landed(erf.at[pl.ds(0, 7)], out_sem.at[8])
 
 
 def body(fields, profiles, phase):
     square, twist = tables()
     dma = pltpu.SemaphoreType.DMA
-    any_spec = pl.BlockSpec(memory_space=pl.ANY)
+    hbm_spec = pl.BlockSpec(memory_space=pltpu.HBM)
     out = pl.pallas_call(
         kernel,
         out_shape=jax.ShapeDtypeStruct((128, 128), F32),
-        in_specs=[any_spec] * 5,
+        in_specs=[hbm_spec] * 5,
         out_specs=pl.BlockSpec(memory_space=pltpu.VMEM),
         scratch_shapes=[
             pltpu.VMEM((128, 128), F32),
@@ -361,7 +347,6 @@
             pltpu.VMEM((8, 2, 4, 4, 16, 128), F32),
             pltpu.VMEM((8, 2, 4, 4, 16, 128), BF16),
             pltpu.VMEM((8, 3, 2, 4, 16, 128), BF16),
-            pltpu.VMEM((8, 128), F32),
             pltpu.VMEM((8, 2, 4, 16, 128), BF16),
             pltpu.VMEM((8, 3, 2, 16, 128), BF16),
             pltpu.VMEM((8, 2, 4, 16, 128), F32),
@@ -370,17 +355,10 @@
             pltpu.VMEM((8, 16, 128), BF16),
             pltpu.VMEM((8, 16, 128), F32),
             pltpu.VMEM((8, 16, 128), BF16),
-            dma((5,)),
-            dma((16,)), dma((16,)),
-            dma((8,)), dma((8,)),
-            dma((16,)), dma((16,)),
-            dma((8, 6)), dma((8, 6)),
-            dma((8, 6)), dma((8, 6)),
-            dma((8,)), dma((8,)),
-            dma((8,)), dma((8,)),
+            dma((5,)), dma((9,)), dma((8,)), dma((1,)), dma((1,)), dma((8, 2)), dma((8, 2)), dma((2,)),
         ],
         compiler_params=pltpu.CompilerParams(
-            collective_id=0, has_side_effects=True, vmem_limit_bytes=40 * 1024 * 1024
+            collective_id=0, has_side_effects=True, vmem_limit_bytes=67_043_328
         ),
     )(fields.reshape(128, 128), profiles, phase.reshape(8, 128), jnp.asarray(square), jnp.asarray(twist))
     return out.reshape(8, 8, 2, 128)

time: 59.7 us -> 46.2 us (0.77)
  Pallas kernels: 54.4 us -> 44.6 us
  local copies, waits for them, and re-layouts: 5.07 us -> 1.47 us
    pallas_call x1, Pallas kernels: 54.4 us -> 44.6 us  [body(): pl.pallas_call(kernel, out_shape=jax.ShapeDtypeStruct((128, 128), F32), i...]
    unnamed x11 -> x1, local copies, waits for them, and re-layouts: 5.07 us -> 1.47 us
where the time goes in v2:
time: 46.2 us; the launch traced here: 46.1 us
  Pallas kernels  44.6 us (97%)
  local copies, waits for them, and re-layouts  1.47 us (3%)
    pallas_call x1, Pallas kernels, body(): pl.pallas_call(kernel, out_shape=jax.ShapeDtypeStruct((128, 128), F32), i...  44.6 us
    unnamed x1, local copies, waits for them, and re-layouts  1.47 us

profile of v2, /device:TPU:1, one launch (start us, length us, event | category | flops | bytes accessed | tf_op | source)
XLA Modules:
  0.0 46.1 jit_solution(7756601659913435335)
XLA Ops:
  0.0 44.6 %shard_map.55 = f32[128,128]{1,0:T(8,128)} custom-call(f32[128,128]{1,0:T(8,128)} %bitcast.4, bf16[2048,256]{1,0:T(8,128)(2,1)} %p_hbm.1, f32[8,128]{1,0:T(8,128)} %bitcast.5, bf16[3,256,256]{2,1,0:T(8,128)(2,1)} %constant.4.clone.sq_hbm, f32[16,128]{1,0:T(8,128)} %constant.5.clone.tw_hbm), custom_call_target="tpu_custom_call" | custom-call | tf_op jit(solution)/shard_map/pallas_call | solution.py:327
  44.6 1.5 %copy.7 = f32[8,8,2,128]{3,2,1,0:T(2,128)} copy(f32[8,8,2,128]{3,2,1,0:T(2,128)} %bitcast.3) | data formatting | bytes 131072

commit v3 on v2

--- a/solution.py
+++ b/solution.py
@@ -14,7 +14,13 @@
 BF16 = jnp.bfloat16
 
 SLOTS = ((2, 0), (2, 1), (1, 0), (1, 1), (3, 0), (3, 1), (0, 1), (0, 0))
-TILE = 512
+TILE = 256
+STRAIGHT_IN = (0, 1)
+STRAIGHT_OUT = (7,)
+GROUPS = ((0,), (1,), (2,), (3,), (4,), (5,), (6,), (7,))
+FIRST_ORDER = (2, 3, 0, 1, 4, 5, 6, 7)
+EARLY, FIRST_LAG = 2, 4
+FAR_FIRST = (10, 6, 9, 11, 14, 2, 5, 7, 8, 13, 15, 1, 3, 4, 12)
 
 
 def tables():
@@ -73,7 +79,7 @@
 def kernel(
     f_hbm, p_hbm, ph_hbm, sq_hbm, tw_hbm, o_ref,
     f_v, p_v, ph_v, sq_v, tw_v, pm_v, pt_v, mbuf, s_hi, s_lo, a1, lo, cs_s, cs_r,
-    kf, ks, kr1, k1s, kr2, kmid, kx, esf, esb, erf, erb,
+    tile, kf, ks, krd, kr1, k1s, kr2, kmid, kx, esf, esb, erf, erb,
     in_sem, out_sem, a1r, lor, csr, a2r, c1r, e_sem,
 ):
     pix, tm = lax.axis_index("pix"), lax.axis_index("tm")
@@ -97,23 +103,30 @@
             src_ref=src, dst_ref=dst, send_sem=ss, recv_sem=rs, device_id=device, device_id_type=MESH
         )
 
+    def at_plane(k):
+        to_y, to_x = lax.rem(y + k // 4, 4), lax.rem(x + k % 4, 4)
+        return to_y, to_x, (zh * 16 + to_y * 4 + to_x, tm)
+
     def column(o):
         peer = lax.rem(here + o, 16)
         return peer // 8, lax.rem(peer, 8)
 
-    def send(*a):
-        remote(*a).start()
-
-    def landed(ref, sem):
+    sent = [0] * 4
+
+    def send(src, dst, phase, rs, device):
+        remote(src, dst, out_sem.at[phase], rs, device).start()
+        sent[phase] += math.prod(src.shape) * src.dtype.itemsize // 4096
+
+    def landed(tiles, sem):
+        ref = tile.at[pl.ds(0, tiles)]
         pltpu.make_async_copy(ref, ref, sem).wait()
 
     barrier = pltpu.get_barrier_semaphore()
     for o in range(1, 16):
         h, t = column(o)
         pl.semaphore_signal(barrier, inc=1, device_id=at_z(h, t), device_id_type=MESH)
-    for k in range(1, 4):
-        pl.semaphore_signal(barrier, inc=1, device_id=at_x(k), device_id_type=MESH)
-        pl.semaphore_signal(barrier, inc=1, device_id=at_y(k), device_id_type=MESH)
+    for k in range(1, 16):
+        pl.semaphore_signal(barrier, inc=1, device_id=at_plane(k)[2], device_id_type=MESH)
 
     loads = [
         pltpu.make_async_copy(src, dst, in_sem.at[n])
@@ -133,10 +146,10 @@
     a1[here] = s_hi[tm]
     lo[tm] = s_lo[tm]
 
-    pl.semaphore_wait(barrier, 21)
+    pl.semaphore_wait(barrier, 30)
     for o in (8, 7, 9, 6, 10, 5, 11, 4, 12, 3, 13, 2, 14, 1, 15):
         h, t = column(o)
-        send(s_hi.at[t], a1.at[here], out_sem.at[0], a1r.at[tm], at_z(h, t))
+        send(s_hi.at[t], a1.at[here], 0, a1r.at[tm], at_z(h, t))
 
 
     loads[1].wait()
@@ -169,58 +182,68 @@
         pm_v[n] = dot(block, sq_v[0]).astype(BF16)
         pt_v[n] = dot(sq_v[0], block, ((0,), (1,))).astype(BF16)
 
-    for o in range(1, 8):
-        t = lax.rem(tm + o, 8)
-        send(s_lo.at[t], lo.at[tm], out_sem.at[1], lor.at[0], at_z(zh, t))
-    for o in range(1, 16):
-        h, t = column(o)
-        send(cs_s, cs_r.at[mine], out_sem.at[2], csr.at[0], at_z(h, t))
-
     blocks = [lax.rem(zl + step, 4) * 2 + lax.rem(core + c, 2) for step, c in SLOTS]
 
     def first_leg(n):
         a = blocks[n]
-        landed(a1.at[pl.ds(0, 1 if SLOTS[n] == (0, 0) else 2)], a1r.at[a])
+        landed(1 if SLOTS[n] == (0, 0) else 2, a1r.at[a])
         first, second = a1[a].astype(F32), a1[8 + a].astype(F32)
         for c in range(2):
             both = jnp.concatenate([first[8 * c : 8 * c + 8], second[8 * c : 8 * c + 8]], axis=0)
             mbuf[a, c, y, x] = both.astype(BF16)
         piece = mbuf.at[a, :, y, x]
+        if n in STRAIGHT_IN:
+            for k in FAR_FIRST:
+                send(piece, piece, 1, a2r.at[n, 1], at_plane(k)[2])
+            return
         for k in range(1, 4):
-            send(piece, piece, out_sem.at[3], a2r.at[n, 0], at_x(k) if n % 2 == 0 else at_y(k))
+            send(piece, piece, 1, a2r.at[n, 0], at_x(k) if n % 2 == 0 else at_y(k))
 
     def second_leg(n):
         a = blocks[n]
-        landed(kr2.at[n], a2r.at[n, 0])
+        landed(6, a2r.at[n, 0])
         piece = mbuf.at[a, :, y] if n % 2 == 0 else mbuf.at[a, :, :, x]
-        for k in range(1, 4):
-            send(piece, piece, out_sem.at[4], a2r.at[n, 1], at_y(k) if n % 2 == 0 else at_x(k))
-
-    def compute(n):
-        a = blocks[n]
-        landed(kr1.at[n], a2r.at[n, 1])
-        fields = jnp.concatenate([mbuf[a, c].reshape(256, 128) for c in range(2)], axis=1)
-        total = None
-        for t in range(2048 // TILE):
-            spatial = dot(pm_v[t], fields)
-            re, im = spatial[:, :128], spatial[:, 128:]
-            power = re * re + im * im
-            nonlin = jnp.concatenate([power * re, power * im], axis=1).astype(BF16)
-            part = dot(pt_v[t], nonlin)
-            total = part if total is None else total + part
+        for k in (2, 1, 3):
+            send(piece, piece, 1, a2r.at[n, 1], at_y(k) if n % 2 == 0 else at_x(k))
+
+    def spread(n, total):
         for c in range(2):
             half = total[:, 128 * c : 128 * c + 128].reshape(4, 4, 16, 128)
             kf[n, c] = half
             ks[n, c] = half.astype(BF16)
-        for k in range(1, 4):
+        if n in STRAIGHT_OUT:
+            for k in FAR_FIRST:
+                to_y, to_x, to = at_plane(k)
+                send(ks.at[n, :, to_y, to_x], krd.at[STRAIGHT_OUT.index(n), k - 1], 2, c1r.at[n, 0], to)
+            return
+        for k in (2, 1, 3):
             if n % 2 == 0:
                 piece, to = ks.at[n, :, :, lax.rem(x + k, 4)], at_x(k)
             else:
                 piece, to = ks.at[n, :, lax.rem(y + k, 4)], at_y(k)
-            send(piece, kr1.at[n, k - 1], out_sem.at[5], c1r.at[n, 0], to)
+            send(piece, kr1.at[n, k - 1], 2, c1r.at[n, 0], to)
+
+    def compute(slots):
+        pieces = []
+        for n in slots:
+            landed(30 if n in STRAIGHT_IN else 24, a2r.at[n, 1])
+            pieces += [mbuf[blocks[n], c].reshape(256, 128) for c in range(2)]
+        fields = jnp.concatenate(pieces, axis=1)
+        total = None
+        for t in range(2048 // TILE):
+            spatial = dot(pm_v[t], fields)
+            cubes = []
+            for at in range(0, 256 * len(slots), 256):
+                re, im = spatial[:, at : at + 128], spatial[:, at + 128 : at + 256]
+                power = re * re + im * im
+                cubes += [power * re, power * im]
+            part = dot(pt_v[t], jnp.concatenate(cubes, axis=1).astype(BF16))
+            total = part if total is None else total + part
+        for at, n in enumerate(slots):
+            spread(n, total[:, 256 * at : 256 * at + 256])
 
     def reduce_first(n):
-        landed(kr1.at[n], c1r.at[n, 0])
+        landed(24, c1r.at[n, 0])
         total = kf[n, :, :, x] if n % 2 == 0 else kf[n, :, y]
         for k in range(3):
             total = total + kr1[n, k].astype(F32)
@@ -231,33 +254,52 @@
                 piece, to = k1s.at[n, :, lax.rem(y + k, 4)], at_y(k)
             else:
                 piece, to = k1s.at[n, :, lax.rem(x + k, 4)], at_x(k)
-            send(piece, kr2.at[n, k - 1], out_sem.at[6], c1r.at[n, 1], to)
+            send(piece, kr2.at[n, k - 1], 2, c1r.at[n, 1], to)
+
+    def reduce_straight(n):
+        landed(30, c1r.at[n, 0])
+        total = kf[n, :, y, x]
+        for k in range(15):
+            total = total + krd[STRAIGHT_OUT.index(n), k].astype(F32)
+        kx[blocks[n]] = total
 
     def reduce_second(n):
-        landed(kr2.at[n], c1r.at[n, 1])
+        landed(6, c1r.at[n, 1])
         total = kmid[n, :, y] if n % 2 == 0 else kmid[n, :, x]
         for k in range(3):
             total = total + kr2[n, k].astype(F32)
         kx[blocks[n]] = total
 
-    for n in range(8):
+    for n in FIRST_ORDER:
         first_leg(n)
-    for n in range(6):
+    for o in range(1, 8):
+        t = lax.rem(tm + o, 8)
+        send(s_lo.at[t], lo.at[tm], 0, lor.at[0], at_z(zh, t))
+    for o in range(1, 16):
+        h, t = column(o)
+        send(cs_s, cs_r.at[mine], 0, csr.at[0], at_z(h, t))
+    two_legs = [n for n in range(8) if n not in STRAIGHT_IN]
+    out_legs = [n for n in range(8) if n not in STRAIGHT_OUT]
+    for n in two_legs[:EARLY]:
         second_leg(n)
-    for n in range(8):
-        compute(n)
-        if n < 2:
-            second_leg(n + 6)
-        if n >= 4:
-            reduce_first(n - 4)
-    for n in range(4):
-        reduce_second(n)
-        reduce_first(n + 4)
-    for n in range(4, 8):
-        reduce_second(n)
-
-    landed(lo.at[pl.ds(0, 7)], lor.at[0])
-    landed(cs_r.at[pl.ds(0, 240)], csr.at[0])
+    for slots in GROUPS:
+        compute(slots)
+        if slots[0] == 0:
+            for m in two_legs[EARLY:]:
+                second_leg(m)
+        for m in out_legs:
+            if m + FIRST_LAG in slots:
+                reduce_first(m)
+    for m in out_legs:
+        if m + FIRST_LAG > 7:
+            reduce_first(m)
+    for m in out_legs:
+        reduce_second(m)
+    for m in STRAIGHT_OUT:
+        reduce_straight(m)
+
+    landed(7, lor.at[0])
+    landed(30, csr.at[0])
     scale = 1.0 / math.sqrt(65536.0)
     at_low = jnp.where(zh == 0, 1.0, 0.0).astype(F32)
     at_high = 1.0 - at_low
@@ -294,30 +336,23 @@
     for a in range(8):
         low_half = jnp.concatenate([out_re[a][:8], out_im[a][:8]], axis=0)
         high_half = jnp.concatenate([out_re[a][8:], out_im[a][8:]], axis=0)
-        esf[a] = low_half * at_low + high_half * at_high
+        esf[a] = (low_half * at_low + high_half * at_high).astype(BF16)
         esb[a] = (low_half * at_high + high_half * at_low).astype(BF16)
     for o in range(8):
         t = lax.rem(tm + o, 8)
-        send(esb.at[t], erb.at[tm], out_sem.at[7], e_sem.at[0], at_z(other, t))
+        send(esb.at[t], erb.at[tm], 3, e_sem.at[0], at_z(other, t))
     for o in range(1, 8):
         t = lax.rem(tm + o, 8)
-        send(esf.at[t], erf.at[tm], out_sem.at[8], e_sem.at[1], at_z(zh, t))
+        send(esf.at[t], erf.at[tm], 3, e_sem.at[1], at_z(zh, t))
     erf[tm] = esf[tm]
-    landed(erb, e_sem.at[0])
-    landed(erf.at[pl.ds(0, 7)], e_sem.at[1])
+    landed(8, e_sem.at[0])
+    landed(7, e_sem.at[1])
     for b in range(8):
-        value = erf[b] + erb[b].astype(F32)
+        value = erf[b].astype(F32) + erb[b].astype(F32)
         for c in range(2):
             o_ref[pl.ds(2 * b + c, 8, stride=16), :] = value[8 * c : 8 * c + 8]
-    landed(a1.at[pl.ds(0, 15)], out_sem.at[0])
-    landed(lo.at[pl.ds(0, 7)], out_sem.at[1])
-    landed(cs_r.at[pl.ds(0, 240)], out_sem.at[2])
-    landed(kr2, out_sem.at[3])
-    landed(kr1, out_sem.at[4])
-    landed(kr1, out_sem.at[5])
-    landed(kr2, out_sem.at[6])
-    landed(erb, out_sem.at[7])
-    landed(erf.at[pl.ds(0, 7)], out_sem.at[8])
+    for phase in range(4):
+        landed(sent[phase], out_sem.at[phase])
 
 
 def body(fields, profiles, phase):
@@ -344,23 +379,25 @@
             pltpu.VMEM((8, 16, 128), BF16),
             pltpu.VMEM((16, 128), F32),
             pltpu.VMEM((256, 128), F32),
+            pltpu.VMEM((512, 16, 128), BF16),
             pltpu.VMEM((8, 2, 4, 4, 16, 128), F32),
             pltpu.VMEM((8, 2, 4, 4, 16, 128), BF16),
+            pltpu.VMEM((len(STRAIGHT_OUT), 15, 2, 16, 128), BF16),
             pltpu.VMEM((8, 3, 2, 4, 16, 128), BF16),
             pltpu.VMEM((8, 2, 4, 16, 128), BF16),
             pltpu.VMEM((8, 3, 2, 16, 128), BF16),
             pltpu.VMEM((8, 2, 4, 16, 128), F32),
             pltpu.VMEM((8, 2, 16, 128), F32),
-            pltpu.VMEM((8, 16, 128), F32),
-            pltpu.VMEM((8, 16, 128), BF16),
-            pltpu.VMEM((8, 16, 128), F32),
-            pltpu.VMEM((8, 16, 128), BF16),
-            dma((5,)), dma((9,)), dma((8,)), dma((1,)), dma((1,)), dma((8, 2)), dma((8, 2)), dma((2,)),
+            pltpu.VMEM((8, 16, 128), BF16),
+            pltpu.VMEM((8, 16, 128), BF16),
+            pltpu.VMEM((8, 16, 128), BF16),
+            pltpu.VMEM((8, 16, 128), BF16),
+            dma((5,)), dma((4,)), dma((8,)), dma((1,)), dma((1,)), dma((8, 2)), dma((8, 2)), dma((2,)),
         ],
         compiler_params=pltpu.CompilerParams(
-            collective_id=0, has_side_effects=True, vmem_limit_bytes=67_043_328
+            collective_id=0, has_side_effects=True, vmem_limit_bytes=44_000_000
         ),
-    )(fields.reshape(128, 128), profiles, phase.reshape(8, 128), jnp.asarray(square), jnp.asarray(twist))
+    )(*[pltpu.with_memory_space_constraint(v, pltpu.HBM) for v in (fields.reshape(128, 128), profiles, phase.reshape(8, 128), jnp.asarray(square), jnp.asarray(twist))])
     return out.reshape(8, 8, 2, 128)
 
 

time: 46.2 us -> 42.7 us (0.924)
  Pallas kernels: 44.6 us -> 42 us
  local copies, waits for them, and re-layouts: 1.47 us -> 0.63 us
    pallas_call x1, Pallas kernels: 44.6 us -> 42 us  [body(): pl.pallas_call(kernel, out_shape=jax.ShapeDtypeStruct((128, 128), F32), i...]
    unnamed x1, local copies, waits for them, and re-layouts: 1.47 us -> 0.63 us
where the time goes in v3:
time: 42.7 us; the launch traced here: 42.6 us
  Pallas kernels  42 us (98%)
  local copies, waits for them, and re-layouts  0.63 us (1%)
    pallas_call x1, Pallas kernels, body(): pl.pallas_call(kernel, out_shape=jax.ShapeDtypeStruct((128, 128), F32), i...  42 us

profile of v3, /device:TPU:1, one launch (start us, length us, event | category | flops | bytes accessed | tf_op | source)
XLA Modules:
  0.0 42.6 jit_solution(1470378540945585121)
XLA Ops:
  0.0 42.0 %shard_map.55 = f32[128,128]{1,0:T(8,128)S(1)} custom-call(f32[128,128]{1,0:T(8,128)} %bitcast.4, bf16[2048,256]{1,0:T(8,128)(2,1)} %p_hbm.1, f32[8,128]{1,0:T(8,128)} %bitcast.5, bf16[3,256,256]{2,1,0:T(8,128)(2,1)} %constant.4.clone.sq_hbm, f32[16,128]{1,0:T(8,128)} %constant.5.clone.tw_hbm), custom_call_target="tpu_custom_call" | custom-call | tf_op jit(solution)/shard_map/pallas_call | solution.py:362
  42.0 0.6 %copy.7 = f32[8,8,2,128]{3,2,1,0:T(2,128)} copy(f32[8,8,2,128]{3,2,1,0:T(2,128)S(1)} %bitcast.3) | data formatting | bytes 131072

commit v4 on v3

--- a/solution.py
+++ b/solution.py
@@ -13,12 +13,12 @@
 F32 = jnp.float32
 BF16 = jnp.bfloat16
 
-SLOTS = ((2, 0), (2, 1), (1, 0), (1, 1), (3, 0), (3, 1), (0, 1), (0, 0))
+SLOTS = ((2, 1), (2, 0), (1, 1), (1, 0), (3, 1), (3, 0), (0, 1), (0, 0))
 TILE = 256
 STRAIGHT_IN = (0, 1)
-STRAIGHT_OUT = (7,)
+STRAIGHT_OUT = (6, 7)
 GROUPS = ((0,), (1,), (2,), (3,), (4,), (5,), (6,), (7,))
-FIRST_ORDER = (2, 3, 0, 1, 4, 5, 6, 7)
+FIRST_ORDER = (2, 0, 4, 3, 1, 5, 6, 7)
 EARLY, FIRST_LAG = 2, 4
 FAR_FIRST = (10, 6, 9, 11, 14, 2, 5, 7, 8, 13, 15, 1, 3, 4, 12)
 
@@ -182,16 +182,20 @@
         pm_v[n] = dot(block, sq_v[0]).astype(BF16)
         pt_v[n] = dot(sq_v[0], block, ((0,), (1,))).astype(BF16)
 
-    blocks = [lax.rem(zl + step, 4) * 2 + lax.rem(core + c, 2) for step, c in SLOTS]
+    blocks = [lax.rem(zl + step, 4) * 2 + c for step, c in SLOTS]
 
     def first_leg(n):
         a = blocks[n]
-        landed(1 if SLOTS[n] == (0, 0) else 2, a1r.at[a])
+        if n < 6:
+            landed(2, a1r.at[a])
+        elif n == 6:
+            landed(2, a1r.at[zl * 2 + 1 - core])
+            landed(1, a1r.at[tm])
         first, second = a1[a].astype(F32), a1[8 + a].astype(F32)
         for c in range(2):
             both = jnp.concatenate([first[8 * c : 8 * c + 8], second[8 * c : 8 * c + 8]], axis=0)
-            mbuf[a, c, y, x] = both.astype(BF16)
-        piece = mbuf.at[a, :, y, x]
+            mbuf[a, y, x, c] = both.astype(BF16)
+        piece = mbuf.at[a, y, x]
         if n in STRAIGHT_IN:
             for k in FAR_FIRST:
                 send(piece, piece, 1, a2r.at[n, 1], at_plane(k)[2])
@@ -202,32 +206,32 @@
     def second_leg(n):
         a = blocks[n]
         landed(6, a2r.at[n, 0])
-        piece = mbuf.at[a, :, y] if n % 2 == 0 else mbuf.at[a, :, :, x]
+        piece = mbuf.at[a, y] if n % 2 == 0 else mbuf.at[a, :, x]
         for k in (2, 1, 3):
             send(piece, piece, 1, a2r.at[n, 1], at_y(k) if n % 2 == 0 else at_x(k))
 
     def spread(n, total):
         for c in range(2):
             half = total[:, 128 * c : 128 * c + 128].reshape(4, 4, 16, 128)
-            kf[n, c] = half
-            ks[n, c] = half.astype(BF16)
+            kf[n, :, :, c] = half
+            ks[n, :, :, c] = half.astype(BF16)
         if n in STRAIGHT_OUT:
             for k in FAR_FIRST:
                 to_y, to_x, to = at_plane(k)
-                send(ks.at[n, :, to_y, to_x], krd.at[STRAIGHT_OUT.index(n), k - 1], 2, c1r.at[n, 0], to)
+                send(ks.at[n, to_y, to_x], krd.at[STRAIGHT_OUT.index(n), k - 1], 2, c1r.at[n, 0], to)
             return
         for k in (2, 1, 3):
             if n % 2 == 0:
-                piece, to = ks.at[n, :, :, lax.rem(x + k, 4)], at_x(k)
+                piece, to = ks.at[n, :, lax.rem(x + k, 4)], at_x(k)
             else:
-                piece, to = ks.at[n, :, lax.rem(y + k, 4)], at_y(k)
+                piece, to = ks.at[n, lax.rem(y + k, 4)], at_y(k)
             send(piece, kr1.at[n, k - 1], 2, c1r.at[n, 0], to)
 
     def compute(slots):
         pieces = []
         for n in slots:
             landed(30 if n in STRAIGHT_IN else 24, a2r.at[n, 1])
-            pieces += [mbuf[blocks[n], c].reshape(256, 128) for c in range(2)]
+            pieces += [mbuf[blocks[n], :, :, c].reshape(256, 128) for c in range(2)]
         fields = jnp.concatenate(pieces, axis=1)
         total = None
         for t in range(2048 // TILE):
@@ -244,28 +248,28 @@
 
     def reduce_first(n):
         landed(24, c1r.at[n, 0])
-        total = kf[n, :, :, x] if n % 2 == 0 else kf[n, :, y]
+        total = kf[n, :, x] if n % 2 == 0 else kf[n, y]
         for k in range(3):
             total = total + kr1[n, k].astype(F32)
         kmid[n] = total
         k1s[n] = total.astype(BF16)
         for k in range(1, 4):
             if n % 2 == 0:
-                piece, to = k1s.at[n, :, lax.rem(y + k, 4)], at_y(k)
+                piece, to = k1s.at[n, lax.rem(y + k, 4)], at_y(k)
             else:
-                piece, to = k1s.at[n, :, lax.rem(x + k, 4)], at_x(k)
+                piece, to = k1s.at[n, lax.rem(x + k, 4)], at_x(k)
             send(piece, kr2.at[n, k - 1], 2, c1r.at[n, 1], to)
 
     def reduce_straight(n):
         landed(30, c1r.at[n, 0])
-        total = kf[n, :, y, x]
+        total = kf[n, y, x]
         for k in range(15):
             total = total + krd[STRAIGHT_OUT.index(n), k].astype(F32)
         kx[blocks[n]] = total
 
     def reduce_second(n):
         landed(6, c1r.at[n, 1])
-        total = kmid[n, :, y] if n % 2 == 0 else kmid[n, :, x]
+        total = kmid[n, y] if n % 2 == 0 else kmid[n, x]
         for k in range(3):
             total = total + kr2[n, k].astype(F32)
         kx[blocks[n]] = total
@@ -372,7 +376,7 @@
             pltpu.VMEM((16, 128), F32),
             pltpu.VMEM((2048 // TILE, TILE, 256), BF16),
             pltpu.VMEM((2048 // TILE, 256, TILE), BF16),
-            pltpu.VMEM((8, 2, 4, 4, 16, 128), BF16),
+            pltpu.VMEM((8, 4, 4, 2, 16, 128), BF16),
             pltpu.VMEM((8, 16, 128), BF16),
             pltpu.VMEM((8, 16, 128), BF16),
             pltpu.VMEM((16, 16, 128), BF16),
@@ -380,13 +384,13 @@
             pltpu.VMEM((16, 128), F32),
             pltpu.VMEM((256, 128), F32),
             pltpu.VMEM((512, 16, 128), BF16),
-            pltpu.VMEM((8, 2, 4, 4, 16, 128), F32),
-            pltpu.VMEM((8, 2, 4, 4, 16, 128), BF16),
+            pltpu.VMEM((8, 4, 4, 2, 16, 128), F32),
+            pltpu.VMEM((8, 4, 4, 2, 16, 128), BF16),
             pltpu.VMEM((len(STRAIGHT_OUT), 15, 2, 16, 128), BF16),
-            pltpu.VMEM((8, 3, 2, 4, 16, 128), BF16),
-            pltpu.VMEM((8, 2, 4, 16, 128), BF16),
+            pltpu.VMEM((8, 3, 4, 2, 16, 128), BF16),
+            pltpu.VMEM((8, 4, 2, 16, 128), BF16),
             pltpu.VMEM((8, 3, 2, 16, 128), BF16),
-            pltpu.VMEM((8, 2, 4, 16, 128), F32),
+            pltpu.VMEM((8, 4, 2, 16, 128), F32),
             pltpu.VMEM((8, 2, 16, 128), F32),
             pltpu.VMEM((8, 16, 128), BF16),
             pltpu.VMEM((8, 16, 128), BF16),

time: 42.7 us -> 42.1 us (0.986)
  Pallas kernels: 42 us -> 41.4 us
    pallas_call x1, Pallas kernels: 42 us -> 41.4 us  [body(): pl.pallas_call(kernel, out_shape=jax.ShapeDtypeStruct((128, 128), F32), i...]
where the time goes in v4:
time: 42.1 us; the launch traced here: 42 us
  Pallas kernels  41.4 us (98%)
  local copies, waits for them, and re-layouts  0.63 us (1%)
    pallas_call x1, Pallas kernels, body(): pl.pallas_call(kernel, out_shape=jax.ShapeDtypeStruct((128, 128), F32), i...  41.4 us

profile of v4, /device:TPU:1, one launch (start us, length us, event | category | flops | bytes accessed | tf_op | source)
XLA Modules:
  0.0 42.0 jit_solution(14578109725917075245)
XLA Ops:
  0.0 41.4 %shard_map.55 = f32[128,128]{1,0:T(8,128)S(1)} custom-call(f32[128,128]{1,0:T(8,128)} %bitcast.4, bf16[2048,256]{1,0:T(8,128)(2,1)} %p_hbm.1, f32[8,128]{1,0:T(8,128)} %bitcast.5, bf16[3,256,256]{2,1,0:T(8,128)(2,1)} %constant.4.clone.sq_hbm, f32[16,128]{1,0:T(8,128)} %constant.5.clone.tw_hbm), custom_call_target="tpu_custom_call" | custom-call | tf_op jit(solution)/shard_map/pallas_call | solution.py:366
  41.4 0.6 %copy.7 = f32[8,8,2,128]{3,2,1,0:T(2,128)} copy(f32[8,8,2,128]{3,2,1,0:T(2,128)S(1)} %bitcast.3) | data formatting | bytes 131072

commit v5 on v4

--- a/solution.py
+++ b/solution.py
@@ -18,7 +18,7 @@
 STRAIGHT_IN = (0, 1)
 STRAIGHT_OUT = (6, 7)
 GROUPS = ((0,), (1,), (2,), (3,), (4,), (5,), (6,), (7,))
-FIRST_ORDER = (2, 0, 4, 3, 1, 5, 6, 7)
+FIRST_ORDER = (0, 2, 4, 3, 1, 5, 6, 7)
 EARLY, FIRST_LAG = 2, 4
 FAR_FIRST = (10, 6, 9, 11, 14, 2, 5, 7, 8, 13, 15, 1, 3, 4, 12)
 
@@ -122,7 +122,7 @@
         pltpu.make_async_copy(ref, ref, sem).wait()
 
     barrier = pltpu.get_barrier_semaphore()
-    for o in range(1, 16):
+    for o in (8, 7, 9, 6, 10, 5, 11, 4, 12, 3, 13, 2, 14, 1, 15):
         h, t = column(o)
         pl.semaphore_signal(barrier, inc=1, device_id=at_z(h, t), device_id_type=MESH)
     for k in range(1, 16):

time: 42.1 us -> 41.8 us (level)
  no operation moved by 1% of the time
where the time goes in v5:
time: 41.8 us; the launch traced here: 41.7 us
  Pallas kernels  41.1 us (98%)
  local copies, waits for them, and re-layouts  0.63 us (2%)
    pallas_call x1, Pallas kernels, body(): pl.pallas_call(kernel, out_shape=jax.ShapeDtypeStruct((128, 128), F32), i...  41.1 us

profile of v5, /device:TPU:1, one launch (start us, length us, event | category | flops | bytes accessed | tf_op | source)
XLA Modules:
  0.0 41.7 jit_solution(13289192238226399327)
XLA Ops:
  0.0 41.1 %shard_map.55 = f32[128,128]{1,0:T(8,128)S(1)} custom-call(f32[128,128]{1,0:T(8,128)} %bitcast.4, bf16[2048,256]{1,0:T(8,128)(2,1)} %p_hbm.1, f32[8,128]{1,0:T(8,128)} %bitcast.5, bf16[3,256,256]{2,1,0:T(8,128)(2,1)} %constant.4.clone.sq_hbm, f32[16,128]{1,0:T(8,128)} %constant.5.clone.tw_hbm), custom_call_target="tpu_custom_call" | custom-call | tf_op jit(solution)/shard_map/pallas_call | solution.py:366
  41.1 0.6 %copy.7 = f32[8,8,2,128]{3,2,1,0:T(2,128)} copy(f32[8,8,2,128]{3,2,1,0:T(2,128)S(1)} %bitcast.3) | data formatting | bytes 131072

commit v6 on v5

--- a/solution.py
+++ b/solution.py
@@ -19,7 +19,7 @@
 STRAIGHT_OUT = (6, 7)
 GROUPS = ((0,), (1,), (2,), (3,), (4,), (5,), (6,), (7,))
 FIRST_ORDER = (0, 2, 4, 3, 1, 5, 6, 7)
-EARLY, FIRST_LAG = 2, 4
+EARLY, FIRST_LAG = 1, 4
 FAR_FIRST = (10, 6, 9, 11, 14, 2, 5, 7, 8, 13, 15, 1, 3, 4, 12)
 
 

time: 41.8 us -> 42.7 us (1.022)
  Pallas kernels: 41.1 us -> 42 us
    pallas_call x1, Pallas kernels: 41.1 us -> 42 us  [body(): pl.pallas_call(kernel, out_shape=jax.ShapeDtypeStruct((128, 128), F32), i...]
where the time goes in v6:
time: 42.7 us
  Pallas kernels  42 us (98%)
  local copies, waits for them, and re-layouts  0.63 us (1%)
    pallas_call x1, Pallas kernels, body(): pl.pallas_call(kernel, out_shape=jax.ShapeDtypeStruct((128, 128), F32), i...  42 us

profile of v6, /device:TPU:1, one launch (start us, length us, event | category | flops | bytes accessed | tf_op | source)
XLA Modules:
  0.0 42.7 jit_solution(10996944162295283649)
XLA Ops:
  0.0 42.0 %shard_map.55 = f32[128,128]{1,0:T(8,128)S(1)} custom-call(f32[128,128]{1,0:T(8,128)} %bitcast.4, bf16[2048,256]{1,0:T(8,128)(2,1)} %p_hbm.1, f32[8,128]{1,0:T(8,128)} %bitcast.5, bf16[3,256,256]{2,1,0:T(8,128)(2,1)} %constant.4.clone.sq_hbm, f32[16,128]{1,0:T(8,128)} %constant.5.clone.tw_hbm), custom_call_target="tpu_custom_call" | custom-call | tf_op jit(solution)/shard_map/pallas_call | solution.py:366
  42.0 0.6 %copy.7 = f32[8,8,2,128]{3,2,1,0:T(2,128)} copy(f32[8,8,2,128]{3,2,1,0:T(2,128)S(1)} %bitcast.3) | data formatting | bytes 131072
